TPU v7x, 32 devices: a whole 2x2x4 slice. The times are simulated.
32 devices in a mesh: days: 2 (over y), sta: 8 (over z, x), win: 2 (over core).
Axes of the slice: x: 2, y: 2, z: 4, core: 2. Of those that a mesh axis runs over, the one named last changes fastest.
Arguments:
- phases: bfloat16 [48, 2048, 16], P(('days', 'win'), 'sta'), parts along dimension 0, may hold values from -3.140625 to 3.140625
- window_valid: int32 [48], P('days'), parts along dimension 0, may hold values 0 or 1
- freq_taper: float32 [2048], replicated, may hold values from 0.1 to 1.9
- pair_mask: int32 [8, 8], replicated, may hold values from 0 to 1, as said below
Outputs:
- correlations: float32 [32, 16, 512], P(('days', 'sta'), None, 'win'), parts along dimension 0
There are 2 independent parts, one for each index of `days`. A program takes and returns all parts, laid end to end along the dimension named above; an argument that names none is the same for every part. Nothing has to cross between parts.
Inputs may be any that keep to these rules, and one draw needn't show every extreme that they name: `pair_mask`: symmetric over the two block indices; every diagonal block is kept.
All inputs are finite; a program needn't handle non-finite values.
Results may differ from a plain program's by a relative error of at most 0.005.
Values may be sent and summed in bfloat16 or wider, within the bound.
A program may use at most 64 MiB of HBM per device.

v0:
```python
import math
import jax
import jax.numpy as jnp
from jax import lax
from jax.sharding import PartitionSpec as P

LAGS = 512


def lag_table(freq_bins, lag_count):
    freq_index = jnp.arange(freq_bins, dtype=jnp.int32)[:, None]
    lag_index = jnp.arange(lag_count, dtype=jnp.int32)[None, :] - lag_count // 2
    wrapped = jnp.mod(freq_index * lag_index, 2 * freq_bins)
    angle = wrapped.astype(jnp.float32) * (math.pi / freq_bins)
    return jnp.stack((jnp.cos(angle), -jnp.sin(angle))).astype(jnp.bfloat16)


def per_device(phases, window_valid, freq_taper, pair_mask):
    sta_count = lax.axis_size("sta")
    win_rows, band_bins, stations = phases.shape
    freq_bins = band_bins * sta_count
    recv_rows = stations // sta_count
    sta_index = lax.axis_index("sta")
    win_group = lax.axis_index("win")
    valid_count = jnp.sum(window_valid.astype(jnp.float32))
    norm_scale = 1.0 / jnp.sqrt(freq_bins * jnp.maximum(valid_count, 1.0))
    bin_weight = freq_taper * norm_scale
    group_valid = lax.dynamic_slice_in_dim(window_valid, win_group * win_rows, win_rows)
    group_weight = group_valid.astype(jnp.bfloat16)[:, None, None]
    own_f = phases.astype(jnp.float32)
    own_cos = jnp.cos(own_f).astype(jnp.bfloat16)
    own_sin = jnp.sin(own_f).astype(jnp.bfloat16)
    left_cos = own_cos * group_weight
    left_sin = own_sin * group_weight
    band_weight = lax.dynamic_slice_in_dim(bin_weight, sta_index * band_bins, band_bins)
    pair_re = jnp.einsum("wki,wkj->ijk", left_cos, own_cos, preferred_element_type=jnp.float32)
    pair_re = pair_re + jnp.einsum(
        "wki,wkj->ijk", left_sin, own_sin, preferred_element_type=jnp.float32
    )
    band_re = (pair_re * band_weight).astype(jnp.bfloat16)
    pair_im = jnp.einsum("wki,wkj->ijk", left_sin, own_cos, preferred_element_type=jnp.float32)
    pair_im = pair_im - jnp.einsum(
        "wki,wkj->ijk", left_cos, own_sin, preferred_element_type=jnp.float32
    )
    band_im = (pair_im * band_weight).astype(jnp.bfloat16)
    spectra = lax.all_to_all(
        jnp.stack((band_re, band_im)), "sta", split_axis=1, concat_axis=3, tiled=True
    )
    lag_count = LAGS
    transform = lag_table(freq_bins, lag_count)
    flat_spectra = spectra.reshape(2, recv_rows * stations, freq_bins)
    correlation = jnp.einsum(
        "cnk,ckt->nt", flat_spectra, transform, preferred_element_type=jnp.float32
    )
    block_row = lax.dynamic_index_in_dim(pair_mask, sta_index, 0, keepdims=False)
    station_row = jnp.repeat(block_row, recv_rows).astype(jnp.float32)
    receiver = sta_index * recv_rows + jnp.arange(recv_rows, dtype=jnp.int32)
    distinct = (receiver[:, None] != jnp.arange(stations, dtype=jnp.int32)[None, :]).astype(
        jnp.float32
    )
    pair_keep = station_row[None, :] * distinct
    correlation = correlation.reshape(recv_rows, stations, lag_count) * pair_keep[:, :, None]
    return lax.psum_scatter(correlation, "win", scatter_dimension=2, tiled=True)


def solution(mesh):
    return jax.shard_map(
        per_device,
        mesh=mesh,
        in_specs=(P(("days", "win"), "sta", None), P("days"), P(), P()),
        out_specs=P(("days", "sta"), None, "win"),
        check_vma=False,
    )
```

profile of v0, /device:TPU:0, one launch (start us, length us, event | category | flops | bytes accessed | tf_op | source)
XLA Modules:
  0.0 74.8 jit_solution(9505695054169387936)
XLA Ops:
  6.5 1.3 %convert_reduce_fusion = f32[]{:T(128)} fusion(s32[24]{0:T(128)} %param.5), kind=kLoop, calls=%fused_computation.32 | loop fusion | flops 47 | bytes 100 | tf_op jit(solution)/shard_map/reduce_sum | solution.py:25
  8.5 0.7 dynamic-slice_convert_fusion
  9.2 1.6 %fusion.12 = (bf16[12,256,16]{1,2,0:T(8,128)(2,1)S(1)}, bf16[12,256,16]{1,2,0:T(8,128)(2,1)S(1)}) fusion(bf16[12,256,16]{1,2,0:T(8,128)(2,1)} %param.4), kind=kLoop, calls=%fused_computation.24 | loop fusion | flops 147456 | bytes 294912 | tf_op jit(solution)/shard_map/convert_element_type | solution.py:32
  10.8 1.6 %broadcast_multiply_fusion.1 = (bf16[12,256,16]{1,2,0:T(8,128)(2,1)S(1)}, bf16[12,256,16]{1,2,0:T(8,128)(2,1)S(1)}) fusion(bf16[12]{0:T(256)(128)(2,1)S(1)} %dynamic-slice_convert_fusion, bf16[12,256,16]{1,2,0:T(8,128)(2,1)} %param.4), kind=kLoop, calls=%fused_computation.26 | loop fusion | flops 491520 | bytes 294936 | tf_op jit(solution)/shard_map/mul | solution.py:33
  12.4 1.0 %copy.35 = bf16[12,256,16]{0,2,1:T(8,128)(2,1)S(1)} copy(bf16[12,256,16]{1,2,0:T(8,128)(2,1)S(1)} %get-tuple-element.5) | data formatting | bytes 196608 | tf_op jit(solution)/shard_map/mul | solution.py:33
  13.5 1.9 %copy.36 = bf16[12,256,16]{2,0,1:T(8,128)(2,1)} copy(bf16[12,256,16]{1,2,0:T(8,128)(2,1)S(1)} %get-tuple-element.8) | data formatting | bytes 196608 | tf_op jit(solution)/shard_map/convert_element_type | solution.py:31
  15.4 1.0 %copy.37 = bf16[12,256,16]{0,2,1:T(8,128)(2,1)S(1)} copy(bf16[12,256,16]{1,2,0:T(8,128)(2,1)S(1)} %get-tuple-element.6) | data formatting | bytes 196608 | tf_op jit(solution)/shard_map/mul | solution.py:34
  16.4 0.9 %copy.38 = bf16[12,256,16]{2,0,1:T(8,128)(2,1)S(1)} copy(bf16[12,256,16]{1,2,0:T(8,128)(2,1)S(1)} %get-tuple-element.7) | data formatting | bytes 196608 | tf_op jit(solution)/shard_map/convert_element_type | solution.py:32
  17.3 0.0 copy-start
  17.4 3.3 %fusion.14 = f32[256,16,16]{2,1,0:T(8,128)} fusion(bf16[12,256,16]{0,2,1:T(8,128)(2,1)S(1)} %copy.35, bf16[12,256,16]{2,0,1:T(8,128)(2,1)} %copy.36), kind=kOutput, calls=%fused_computation.35 | convolution fusion | flops 1572864 | bytes 458752 | tf_op jit(solution)/shard_map/wki,wkj->ijk/dot_general | solution.py:36
  20.7 0.0 copy-done
  20.7 2.0 %fusion.15 = f32[256,16,16]{2,1,0:T(8,128)} fusion(bf16[12,256,16]{0,2,1:T(8,128)(2,1)S(1)} %copy.37, bf16[12,256,16]{2,0,1:T(8,128)(2,1)S(1)} %copy-done), kind=kOutput, calls=%fused_computation.36 | convolution fusion | flops 1572864 | bytes 458752 | tf_op jit(solution)/shard_map/wki,wkj->ijk/dot_general | solution.py:41
  22.7 0.8 %dynamic-slice_multiply_fusion = f32[256]{0:T(256)S(1)} fusion(f32[2048]{0:T(1024)} %param.6, s32[]{:T(128)S(6)} %select_n.31, f32[]{:T(128)S(6)} %sqrt.3), kind=kLoop, calls=%fused_computation.29 | loop fusion | flops 256 | bytes 2056 | tf_op jit(solution)/shard_map/mul | solution.py:27
  23.4 0.0 copy-start.1
  23.4 2.4 %fusion.7 = bf16[1,16,16,256]{2,1,3,0:T(8,128)(2,1)S(1)} fusion(f32[256,16,16]{2,1,0:T(8,128)} %fusion.14, bf16[12,256,16]{0,2,1:T(8,128)(2,1)S(1)} %copy.37, bf16[12,256,16]{2,0,1:T(8,128)(2,1)S(1)} %copy.38, f32[256]{0:T(256)S(1)} %dynamic-slice_multiply_fusion), kind=kOutput, calls=%fused_computation.16 | convolution fusion | flops 1769472 | bytes 590848 | tf_op jit(solution)/shard_map/wki,wkj->ijk/dot_general | solution.py:37
  25.9 0.0 copy-done.1
  25.9 0.7 fusion.8
  26.6 0.5 pad_maximum_fusion
  27.0 2.3 %copy.43 = bf16[2,16,16,256]{3,2,0,1:T(8,128)(2,1)} copy(bf16[2,16,16,256]{2,1,3,0:T(8,128)(2,1)S(1)} %pad_maximum_fusion) | data formatting | bytes 524288 | tf_op jit(solution)/shard_map/stack | solution.py:47
  29.3 7.3 %all-to-all-start = ((bf16[2,16,16,256]{3,2,0,1:T(8,128)(2,1)}), bf16[2,16,16,256]{3,2,0,1:T(8,128)(2,1)S(1)}, u32[]{:S(2)}, u32[]{:S(2)}) async-start(bf16[2,16,16,256]{3,2,0,1:T(8,128)(2,1)} %copy.43), calls=%async_computation | async-start | bytes 524288 | tf_op jit(solution)/shard_map/all_to_all | solution.py:46
  36.6 0.0 reduce-scatter.2.cloned.1.call-start
  36.7 0.7 convert_bitcast_fusion
  37.4 0.1 broadcast_in_dim.2
  37.4 0.1 convert_element_type.71
  37.5 0.1 compare_select_fusion
  37.6 18.1 %cosine_convert_fusion = (bf16[1,2048,512]{2,1,0:T(8,128)(2,1)S(1)}, bf16[1,2048,512]{2,1,0:T(8,128)(2,1)}) fusion(s32[512]{0:T(512)S(1)} %iota_add_fusion), kind=kLoop, calls=%fused_computation.8 | loop fusion | flops 17825792 | bytes 4196352 | tf_op jit(solution)/shard_map/convert
  55.7 0.0 all-to-all-done
  55.7 0.1 copy.47
  55.9 0.1 reshape.160
  56.0 2.9 %fusion.10 = f32[2,16,512]{2,1,0:T(8,128)} fusion(bf16[2,16,2,2048]{3,1,0,2:T(8,128)(2,1)S(1)} %bitcast.43, bf16[1,2048,512]{2,1,0:T(8,128)(2,1)} %get-tuple-element.10, bf16[1,2048,512]{2,1,0:T(8,128)(2,1)S(1)} %get-tuple-element.9, f32[2,16]{1,0:T(2,128)S(1)} %compare_select_fusion), kind=kOutput, calls=%fused_computation.19 | convolution fusion | flops 136331264 | bytes 4522112 | tf_op jit(solution)/shard_map/cnk,ckt->nt/dot_general | solution.py:52
  58.9 0.0 reduce-scatter.2.cloned.1.call-update
  58.9 9.1 %reduce-scatter.2.cloned.1.call-done = f32[2,16,256]{2,1,0:T(8,128)} async-done(((f32[2,16,512]{2,1,0:T(8,128)}), f32[2,16,256]{2,1,0:T(8,128)}) %reduce-scatter.2.cloned.1.call-update) | async-done | bytes 32784 | tf_op jit(solution)/shard_map/reduce_scatter | solution.py:63
  (2 shorter events, 0.0 us)
Async XLA Ops:
  17.3 3.3 %copy-start = (bf16[12,256,16]{2,0,1:T(8,128)(2,1)S(1)}, bf16[12,256,16]{2,0,1:T(8,128)(2,1)}, u32[]{:S(2)}) copy-start(bf16[12,256,16]{2,0,1:T(8,128)(2,1)} %copy.36) | copy-start | bytes 294916
  23.4 2.4 %copy-start.1 = (f32[256,16,16]{2,1,0:T(8,128)S(1)}, f32[256,16,16]{2,1,0:T(8,128)}, u32[]{:S(2)}) copy-start(f32[256,16,16]{2,1,0:T(8,128)} %fusion.15) | copy-start | bytes 786436
  29.3 26.4 %all-to-all-start = ((bf16[2,16,16,256]{3,2,0,1:T(8,128)(2,1)}), bf16[2,16,16,256]{3,2,0,1:T(8,128)(2,1)S(1)}, u32[]{:S(2)}, u32[]{:S(2)}) async-start(bf16[2,16,16,256]{3,2,0,1:T(8,128)(2,1)} %copy.43), calls=%async_computation | async-start | bytes 524288 | tf_op jit(solution)/shard_map/all_to_all | solution.py:46
  36.6 31.4 %reduce-scatter.2.cloned.1.call-start = ((), (), s32[]{:S(2)}) async-start(), calls=%async_computation.2 | async-start | bytes 98304 | tf_op jit(solution)/shard_map/reduce_scatter | solution.py:63
Sparse Core Ops, SparseCore 0:
  59.1 8.8 reduce-scatter.1
where the time goes:
time: 75.3 us; the launch traced here: 74.8 us
  other arithmetic  25.3 us (34%)
  between operations  14.2 us (19%)
  matrix products  11.3 us (15%)
  waiting for transfers between devices  9.08 us (12%)
  local copies, waits for them, and re-layouts  7.59 us (10%)
  starting transfers between devices  7.31 us (10%)
    another operation x1, other arithmetic  18.1 us
    reduce_scatter x1, waiting for transfers between devices, per_device(): return lax.psum_scatter(correlation, 'win', scatter_dimension=2, tiled=True)  9.07 us
    all_to_all x1, starting transfers between devices, per_device(): lax.all_to_all(jnp.stack((band_re, band_im)), 'sta', split_axis=1, concat...  7.28 us
    dot_general x1, matrix products, per_device(): jnp.einsum('wki,wkj->ijk', left_cos, own_cos, preferred_element_type=jnp....  3.32 us
    dot_general x1, matrix products, per_device(): jnp.einsum('cnk,ckt->nt', flat_spectra, transform, preferred_element_type...  2.92 us
    dot_general x1, matrix products, per_device(): jnp.einsum('wki,wkj->ijk', left_sin, own_sin, preferred_element_type=jnp....  2.42 us
    another operation x1, local copies, waits for them, and re-layouts, per_device(): jnp.stack((band_re, band_im))  2.28 us
    dot_general x1, matrix products, per_device(): jnp.einsum('wki,wkj->ijk', left_sin, own_cos, preferred_element_type=jnp....  1.98 us
  transfers between devices with their start and end apart: 2, of which 1 were waited for; matrix products, arithmetic and copies ran while one was open for 25% of the time, Pallas kernels for 0%

commit v1 on v0

--- a/solution.py
+++ b/solution.py
@@ -43,9 +43,10 @@
         "wki,wkj->ijk", left_cos, own_sin, preferred_element_type=jnp.float32
     )
     band_im = (pair_im * band_weight).astype(jnp.bfloat16)
-    spectra = lax.all_to_all(
-        jnp.stack((band_re, band_im)), "sta", split_axis=1, concat_axis=3, tiled=True
-    )
+    part = jnp.stack((band_re, band_im))
+    cells = jnp.split(part, lax.axis_size("sta"), axis=1)
+    got = lax.all_to_all(jnp.stack(cells), "sta", 0, 0)
+    spectra = jnp.concatenate(got, axis=3)
     lag_count = LAGS
     transform = lag_table(freq_bins, lag_count)
     flat_spectra = spectra.reshape(2, recv_rows * stations, freq_bins)

time: 75.3 us -> 82.6 us (1.097)
  other arithmetic: 25.3 us -> 29.7 us
  matrix products: 11.3 us -> 13.8 us
    unnamed x0 -> x7, other arithmetic: none -> 4.23 us
    dot_general x1, matrix products: 0.68 us -> 2.27 us  [per_device(): jnp.einsum('wki,wkj->ijk', left_cos, own_sin, preferred_element_type=jnp....]
    dot_general x1, matrix products: 2.42 us -> 3.28 us  [per_device(): jnp.einsum('wki,wkj->ijk', left_sin, own_sin, preferred_element_type=jnp....]
    another operation x1 -> x3, local copies, waits for them, and re-layouts: 2.28 us -> 2.91 us  [the longest x2 2.79 us: per_device(): part = jnp.stack((band_re, band_im))]
  transfers between devices with their start and end apart: 2 -> 2, of which waited for: 1 -> 1; matrix products, arithmetic and copies ran while one was open for 25% -> 23% of each run, Pallas kernels for 0% -> 0%
where the time goes in v1:
time: 82.6 us; the launch traced here: 82.1 us
  other arithmetic  29.7 us (36%)
  between operations  14.2 us (17%)
  matrix products  13.8 us (17%)
  waiting for transfers between devices  9.08 us (11%)
  local copies, waits for them, and re-layouts  8.07 us (10%)
  starting transfers between devices  7.31 us (9%)
    another operation x1, other arithmetic  18.1 us
    reduce_scatter x1, waiting for transfers between devices, per_device(): return lax.psum_scatter(correlation, 'win', scatter_dimension=2, tiled=True)  9.07 us
    all_to_all x1, starting transfers between devices, per_device(): got = lax.all_to_all(jnp.stack(cells), 'sta', 0, 0)  7.27 us
    unnamed x7, other arithmetic  4.23 us
    dot_general x1, matrix products, per_device(): jnp.einsum('wki,wkj->ijk', left_cos, own_cos, preferred_element_type=jnp....  3.3 us
    dot_general x1, matrix products, per_device(): jnp.einsum('wki,wkj->ijk', left_sin, own_sin, preferred_element_type=jnp....  3.28 us
    dot_general x1, matrix products, per_device(): jnp.einsum('cnk,ckt->nt', flat_spectra, transform, preferred_element_type...  2.9 us
    another operation x2, local copies, waits for them, and re-layouts, per_device(): part = jnp.stack((band_re, band_im))  2.79 us
  transfers between devices with their start and end apart: 2, of which 1 were waited for; matrix products, arithmetic and copies ran while one was open for 23% of the time, Pallas kernels for 0%

profile of v1, /device:TPU:0, one launch (start us, length us, event | category | flops | bytes accessed | tf_op | source)
XLA Modules:
  0.0 82.1 jit_solution(1631424922104727137)
XLA Ops:
  6.5 1.3 %convert_reduce_fusion = f32[]{:T(128)} fusion(s32[24]{0:T(128)} %param.5), kind=kLoop, calls=%fused_computation.61 | loop fusion | flops 47 | bytes 100 | tf_op jit(solution)/shard_map/reduce_sum | solution.py:25
  8.5 0.7 dynamic-slice_convert_fusion
  9.2 1.6 %fusion.12 = (bf16[12,256,16]{1,2,0:T(8,128)(2,1)S(1)}, bf16[12,256,16]{1,2,0:T(8,128)(2,1)S(1)}) fusion(bf16[12,256,16]{1,2,0:T(8,128)(2,1)} %param.4), kind=kLoop, calls=%fused_computation.36 | loop fusion | flops 147456 | bytes 294912 | tf_op jit(solution)/shard_map/convert_element_type | solution.py:32
  10.8 1.6 %broadcast_multiply_fusion.1 = (bf16[12,256,16]{1,2,0:T(8,128)(2,1)S(1)}, bf16[12,256,16]{1,2,0:T(8,128)(2,1)S(1)}) fusion(bf16[12]{0:T(256)(128)(2,1)S(1)} %dynamic-slice_convert_fusion, bf16[12,256,16]{1,2,0:T(8,128)(2,1)} %param.4), kind=kLoop, calls=%fused_computation.38 | loop fusion | flops 491520 | bytes 294936 | tf_op jit(solution)/shard_map/mul | solution.py:33
  12.4 1.0 %copy.23 = bf16[12,256,16]{0,2,1:T(8,128)(2,1)S(1)} copy(bf16[12,256,16]{1,2,0:T(8,128)(2,1)S(1)} %get-tuple-element.5) | data formatting | bytes 196608 | tf_op jit(solution)/shard_map/mul | solution.py:33
  13.5 1.9 %copy.24 = bf16[12,256,16]{2,0,1:T(8,128)(2,1)} copy(bf16[12,256,16]{1,2,0:T(8,128)(2,1)S(1)} %get-tuple-element.8) | data formatting | bytes 196608 | tf_op jit(solution)/shard_map/convert_element_type | solution.py:31
  15.3 1.0 %copy.25 = bf16[12,256,16]{0,2,1:T(8,128)(2,1)S(1)} copy(bf16[12,256,16]{1,2,0:T(8,128)(2,1)S(1)} %get-tuple-element.6) | data formatting | bytes 196608 | tf_op jit(solution)/shard_map/mul | solution.py:34
  16.4 0.9 %copy.26 = bf16[12,256,16]{2,0,1:T(8,128)(2,1)S(1)} copy(bf16[12,256,16]{1,2,0:T(8,128)(2,1)S(1)} %get-tuple-element.7) | data formatting | bytes 196608 | tf_op jit(solution)/shard_map/convert_element_type | solution.py:32
  17.3 0.0 copy-start
  17.3 3.3 %fusion.23 = f32[256,16,16]{2,1,0:T(8,128)} fusion(bf16[12,256,16]{0,2,1:T(8,128)(2,1)S(1)} %copy.23, bf16[12,256,16]{2,0,1:T(8,128)(2,1)} %copy.24), kind=kOutput, calls=%fused_computation.64 | convolution fusion | flops 1572864 | bytes 458752 | tf_op jit(solution)/shard_map/wki,wkj->ijk/dot_general | solution.py:36
  20.6 0.0 copy-done
  20.6 2.0 %fusion.24 = f32[256,16,16]{2,1,0:T(8,128)} fusion(bf16[12,256,16]{0,2,1:T(8,128)(2,1)S(1)} %copy.25, bf16[12,256,16]{2,0,1:T(8,128)(2,1)S(1)} %copy-done), kind=kOutput, calls=%fused_computation.65 | convolution fusion | flops 1572864 | bytes 458752 | tf_op jit(solution)/shard_map/wki,wkj->ijk/dot_general | solution.py:41
  22.6 0.8 dynamic-slice_multiply_fusion
  23.4 3.3 %fusion.7 = bf16[1,16,16,256]{2,1,3,0:T(8,128)(2,1)} fusion(f32[256,16,16]{2,1,0:T(8,128)} %fusion.23, bf16[12,256,16]{0,2,1:T(8,128)(2,1)S(1)} %copy.25, bf16[12,256,16]{2,0,1:T(8,128)(2,1)S(1)} %copy.26, f32[256]{0:T(256)S(1)} %dynamic-slice_multiply_fusion), kind=kOutput, calls=%fused_computation.15 | convolution fusion | flops 1769472 | bytes 590848 | tf_op jit(solution)/shard_map/wki,wkj->ijk/dot_general | solution.py:37
  26.7 2.0 %copy.31 = bf16[1,16,16,256]{3,2,1,0:T(8,128)(2,1)S(1)} copy(bf16[1,16,16,256]{2,1,3,0:T(8,128)(2,1)} %fusion.7) | data formatting | bytes 262144 | tf_op jit(solution)/shard_map/stack | solution.py:46
  28.6 2.3 %fusion.8 = bf16[1,16,16,256]{2,1,3,0:T(8,128)(2,1)S(1)} fusion(f32[256,16,16]{2,1,0:T(8,128)} %fusion.24, bf16[12,256,16]{0,2,1:T(8,128)(2,1)S(1)} %copy.23, bf16[12,256,16]{2,0,1:T(8,128)(2,1)S(1)} %copy.26, f32[256]{0:T(256)S(1)} %dynamic-slice_multiply_fusion), kind=kOutput, calls=%fused_computation.16 | convolution fusion | flops 1769472 | bytes 590848 | tf_op jit(solution)/shard_map/wki,wkj->ijk/dot_general | solution.py:42
  30.9 0.8 %copy.32 = bf16[1,16,16,256]{3,2,1,0:T(8,128)(2,1)S(1)} copy(bf16[1,16,16,256]{2,1,3,0:T(8,128)(2,1)S(1)} %fusion.8) | data formatting | bytes 262144 | tf_op jit(solution)/shard_map/stack | solution.py:46
  31.8 0.6 bitcast_dynamic-update-slice_fusion.6
  32.4 0.6 bitcast_dynamic-update-slice_fusion.5
  33.0 0.6 bitcast_dynamic-update-slice_fusion.4
  33.6 0.6 bitcast_dynamic-update-slice_fusion.3
  34.2 0.6 bitcast_dynamic-update-slice_fusion.2
  34.8 0.6 bitcast_dynamic-update-slice_fusion.1
  35.4 0.6 bitcast_dynamic-update-slice_fusion
  36.0 0.6 fusion.21
  36.6 7.3 %all-to-all-start = ((bf16[8,2,2,16,256]{4,3,2,1,0:T(8,128)(2,1)}), bf16[8,2,2,16,256]{4,3,2,1,0:T(8,128)(2,1)S(1)}, u32[]{:S(2)}, u32[]{:S(2)}) async-start(bf16[8,2,2,16,256]{4,3,2,1,0:T(8,128)(2,1)} %fusion.21), calls=%async_computation | async-start | bytes 524288 | tf_op jit(solution)/shard_map/all_to_all | solution.py:48
  43.9 0.0 reduce-scatter.2.cloned.1.call-start
  43.9 0.7 convert_bitcast_fusion
  44.6 0.1 broadcast_in_dim.2
  44.7 0.1 convert_element_type.71
  44.8 0.1 compare_select_fusion
  44.9 18.1 %cosine_convert_fusion = (bf16[1,2048,512]{2,1,0:T(8,128)(2,1)S(1)}, bf16[1,2048,512]{2,1,0:T(8,128)(2,1)}) fusion(s32[512]{0:T(512)S(1)} %iota_add_fusion), kind=kLoop, calls=%fused_computation.8 | loop fusion | flops 17825792 | bytes 4196352 | tf_op jit(solution)/shard_map/convert
  63.0 0.0 all-to-all-done
  63.0 0.1 copy.33
  63.1 0.1 reshape_reshape.3
  63.3 2.9 %fusion.10 = f32[2,16,512]{2,1,0:T(8,128)} fusion(bf16[2,16,2,2048]{3,1,0,2:T(8,128)(2,1)S(1)} %bitcast.57, bf16[1,2048,512]{2,1,0:T(8,128)(2,1)} %get-tuple-element.10, bf16[1,2048,512]{2,1,0:T(8,128)(2,1)S(1)} %get-tuple-element.9, f32[2,16]{1,0:T(2,128)S(1)} %compare_select_fusion), kind=kOutput, calls=%fused_computation.18 | convolution fusion | flops 136331264 | bytes 4522112 | tf_op jit(solution)/shard_map/cnk,ckt->nt/dot_general | solution.py:53
  66.2 0.0 reduce-scatter.2.cloned.1.call-update
  66.2 9.1 %reduce-scatter.2.cloned.1.call-done = f32[2,16,256]{2,1,0:T(8,128)} async-done(((f32[2,16,512]{2,1,0:T(8,128)}), f32[2,16,256]{2,1,0:T(8,128)}) %reduce-scatter.2.cloned.1.call-update) | async-done | bytes 32784 | tf_op jit(solution)/shard_map/reduce_scatter | solution.py:64
  (2 shorter events, 0.0 us)
Async XLA Ops:
  17.3 3.3 %copy-start = (bf16[12,256,16]{2,0,1:T(8,128)(2,1)S(1)}, bf16[12,256,16]{2,0,1:T(8,128)(2,1)}, u32[]{:S(2)}) copy-start(bf16[12,256,16]{2,0,1:T(8,128)(2,1)} %copy.24) | copy-start | bytes 294916
  36.6 26.4 %all-to-all-start = ((bf16[8,2,2,16,256]{4,3,2,1,0:T(8,128)(2,1)}), bf16[8,2,2,16,256]{4,3,2,1,0:T(8,128)(2,1)S(1)}, u32[]{:S(2)}, u32[]{:S(2)}) async-start(bf16[8,2,2,16,256]{4,3,2,1,0:T(8,128)(2,1)} %fusion.21), calls=%async_computation | async-start | bytes 524288 | tf_op jit(solution)/shard_map/all_to_all | solution.py:48
  43.9 31.4 %reduce-scatter.2.cloned.1.call-start = ((), (), s32[]{:S(2)}) async-start(), calls=%async_computation.2 | async-start | bytes 98304 | tf_op jit(solution)/shard_map/reduce_scatter | solution.py:64
Sparse Core Ops, SparseCore 0:
  66.3 8.8 reduce-scatter.1
